TPU v7x, 32 devices: a whole 2x2x4 slice. The times are simulated.
32 devices in a mesh: row: 16 (over z, y, x), col: 2 (over core).
Axes of the slice: x: 2, y: 2, z: 4, core: 2. Of those that a mesh axis runs over, the one named last changes fastest.
Arguments:
- tokens: bfloat16 [8192, 6144], P('row', 'col'), may hold values from -6 to 6
- w_blocks: bfloat16 [96, 81920], P('col', 'row'), may hold values from -0.25 to 0.25
- hidden_bias: bfloat16 [12288], P('col'), may hold values from -3 to 3
- pattern: int32 [96, 5], replicated, may hold values from 0 to 47, as said below
- grad_act: bfloat16 [8192, 12288], P('row', 'col'), may hold values from -6 to 6
Outputs:
- activation: bfloat16 [8192, 12288], P('row', 'col')
- weight_grad: float32 [96, 81920], P('col', 'row')
- bias_grad: float32 [12288], P('col')
Inputs may be any that keep to these rules, and one draw needn't show every extreme that they name: `pattern`: panel p holds input blocks p * 24 to (p + 1) * 24 - 1, and hidden block h lies in group g = h // 48. Slot 0 of h names a block in panel g; slot k for 1 <= k <= 3 names a block in panel (g + 2^(k-1)) mod 2; slot 4 names one of the blocks 0 to 1. Names may repeat within a hidden block.
All inputs are finite; a program needn't handle non-finite values.
Results may differ from a plain program's by a relative error of at most 0.003.
Values may be sent and summed in bfloat16 or wider, within the bound.
A program may use at most 192 MiB of HBM per device.

v0:
```python
import math

import jax
import jax.numpy as jnp
from jax import lax
from jax.sharding import PartitionSpec as P

BLK = 128
LEVELS = 3
GLOB = 2
KSLOT = 5


def from_behind(block, axis, distance):
    devices = range(lax.axis_size(axis))
    route = [((i - distance) % len(devices), i) for i in devices]
    return lax.ppermute(block, axis, route)


def broadcast(value, axis, source):
    kept = jnp.where(lax.axis_index(axis) == source, value, 0).astype(value.dtype)
    return lax.psum(kept, axis)


def body(tokens, w_blocks, hidden_bias, pattern, grad_act):
    tok_rows = tokens.shape[0]
    local_blocks = w_blocks.shape[0]
    col_count = lax.axis_size("col")
    col_index = lax.axis_index("col")
    panel_blocks = tokens.shape[1] // BLK
    inv_scale = 1.0 / math.sqrt(tok_rows * lax.axis_size("row"))
    gathered_weights = lax.all_gather(w_blocks, "row", axis=1, tiled=True)
    weights = gathered_weights.reshape(local_blocks, KSLOT, BLK, BLK)
    my_pattern = lax.dynamic_slice_in_dim(pattern, col_index * local_blocks, local_blocks, 0)
    own_panel = tokens.reshape(tok_rows, panel_blocks, BLK)
    pieces = [jnp.take(own_panel, my_pattern[:, 0] - col_index * panel_blocks, axis=1)]
    for level_index in range(LEVELS):
        offset = 2**level_index % col_count
        if offset == 0:
            source = own_panel
        else:
            moved = from_behind(tokens, "col", -offset)
            source = moved.reshape(tok_rows, panel_blocks, BLK)
        home_panel = (col_index + offset) % col_count
        pieces.append(
            jnp.take(source, my_pattern[:, level_index + 1] - home_panel * panel_blocks, axis=1)
        )
    shared = broadcast(tokens[:, : GLOB * BLK], "col", 0).reshape(tok_rows, GLOB, BLK)
    pieces.append(jnp.take(shared, my_pattern[:, LEVELS + 1], axis=1))
    picked = jnp.stack(pieces, axis=2)
    pre_act = jnp.einsum("thkc,hkcd->thd", picked, weights, preferred_element_type=jnp.float32)
    pre_act = pre_act + hidden_bias.astype(jnp.float32).reshape(local_blocks, BLK)
    act_value, pull_back = jax.vjp(jax.nn.gelu, pre_act)
    activation = act_value.reshape(tok_rows, local_blocks * BLK).astype(jnp.bfloat16)
    grad_pre = pull_back(grad_act.astype(jnp.float32).reshape(tok_rows, local_blocks, BLK))[0]
    grad_rounded = grad_pre.astype(jnp.bfloat16)
    weight_terms = (
        jnp.einsum("thkc,thd->hkcd", picked, grad_rounded, preferred_element_type=jnp.float32)
        * inv_scale
    )
    weight_terms = weight_terms.reshape(local_blocks, KSLOT * BLK * BLK)
    weight_grad = lax.psum_scatter(weight_terms, "row", scatter_dimension=1, tiled=True)
    bias_terms = jnp.sum(grad_pre, axis=0).reshape(local_blocks * BLK) * inv_scale
    bias_grad = lax.psum(bias_terms, "row")
    return (activation, weight_grad, bias_grad)


def solution(mesh):
    return jax.shard_map(
        body,
        mesh=mesh,
        in_specs=(P("row", "col"), P("col", "row"), P("col"), P(), P("row", "col")),
        out_specs=(P("row", "col"), P("col", "row"), P("col")),
        check_vma=False,
    )
```

profile of v0, /device:TPU:9, one launch (start us, length us, event | category | flops | bytes accessed | tf_op | source)
XLA Modules:
  0.0 449.2 jit_solution(14091707161921270317)
XLA Ops:
  8.0 0.0 copy-start
  8.0 0.0 all-reduce.2.cloned.1.call-start
  8.1 4.7 %copy.17 = bf16[512,3072]{0,1:T(8,128)(2,1)} copy(bf16[512,3072]{1,0:T(8,128)(2,1)} %param.7) | data formatting | bytes 6291456 | tf_op args[0]
  12.8 1.0 slice_select_fusion
  13.7 0.8 copy.24
  14.6 0.0 all-reduce.2.cloned.1.call-update
  14.6 0.0 all-gather.2.cloned.1.call-start
  14.7 0.5 all-gather.2.cloned.1.call-update
  15.2 0.0 reduce-scatter.2.cloned.1.call-start
  15.2 0.7 collective-permute-start
  16.0 3.5 copy.18
  19.5 0.0 copy-done
  19.5 0.1 constant_dynamic-slice_fusion
  19.6 5.0 %gather_fusion.1 = bf16[48,512,128]{2,1,0:T(8,128)(2,1)} fusion(bf16[512,24,128]{2,0,1:T(8,128)(2,1)S(1)} %copy.18, s32[1024]{0:T(1024)S(1)} %pad_clamp_fusion.4), kind=kCustom, calls=%fused_computation.clone | custom fusion | bytes 12583104 | tf_op jit(solution)/shard_map/jit(_take)/gather | solution.py:36
  24.6 5.0 %gather_fusion.3 = bf16[48,512,128]{2,1,0:T(8,128)(2,1)} fusion(bf16[512,24,128]{2,0,1:T(8,128)(2,1)S(1)} %copy.18, s32[1024]{0:T(1024)S(1)} %get-tuple-element.31), kind=kCustom, calls=%fused_computation.2.clone | custom fusion | bytes 12583104 | tf_op jit(solution)/shard_map/jit(_take)/gather | solution.py:46
  29.6 4.9 %gather_fusion.4 = bf16[48,512,128]{2,1,0:T(8,128)(2,1)} fusion(bf16[512,24,128]{2,0,1:T(8,128)(2,1)S(1)} %copy.18, s32[1024]{0:T(1024)S(1)} %get-tuple-element.30), kind=kCustom, calls=%fused_computation.3.clone | custom fusion | bytes 12583104 | tf_op jit(solution)/shard_map/jit(_take)/gather | solution.py:46
  34.5 0.0 copy-start.2
  34.5 9.5 %copy.26 = f32[512,6144]{0,1:T(8,128)} copy(bf16[512,6144]{1,0:T(8,128)(2,1)} %param.11) | data formatting | bytes 18874368 | tf_op jit(solution)/shard_map/reshape | solution.py:55
  44.1 0.0 copy-done.2
  44.1 7.8 %bitcast_dynamic-update-slice_fusion.3 = bf16[512,48,5,128]{3,0,2,1:T(8,128)(2,1)} fusion(bf16[48,512,128]{2,1,0:T(8,128)(2,1)} %gather_fusion.1, pred[48]{0:T(512)(128)(4,1)S(1)} %get-tuple-element.26), kind=kLoop, calls=%fused_computation.27 | loop fusion | flops 3145727 | bytes 12582960
  51.9 0.0 all-reduce.2.cloned.1.call-done
  51.9 5.8 %gather_fusion = bf16[48,512,128]{2,1,0:T(8,128)(2,1)} fusion(bf16[512,2,128]{2,0,1:T(8,128)(2,1)} %all-reduce.2.cloned.1.call-done, s32[1024]{0:T(1024)S(1)} %pad_clamp_fusion), kind=kCustom, calls=%fused_computation.4 | custom fusion | bytes 12583104 | tf_op jit(solution)/shard_map/jit(_take)/gather | solution.py:49
  57.8 0.0 collective-permute-done
  57.8 3.5 copy.20
  61.3 5.0 %gather_fusion.2 = bf16[48,512,128]{2,1,0:T(8,128)(2,1)} fusion(bf16[512,24,128]{2,0,1:T(8,128)(2,1)S(1)} %copy.20, s32[1024]{0:T(1024)S(1)} %pad_clamp_fusion.3), kind=kCustom, calls=%fused_computation.1.clone | custom fusion | bytes 12583104 | tf_op jit(solution)/shard_map/jit(_take)/gather | solution.py:46
  66.3 7.9 %bitcast_dynamic-update-slice_fusion.2 = bf16[512,48,5,128]{3,0,2,1:T(8,128)(2,1)} fusion(bf16[512,48,5,128]{3,0,2,1:T(8,128)(2,1)} %bitcast_dynamic-update-slice_fusion.3, bf16[48,512,128]{2,1,0:T(8,128)(2,1)} %gather_fusion.2, pred[48]{0:T(512)(128)(4,1)S(1)} %get-tuple-element.24), kind=kLoop, calls=%fused_computation.26 | loop fusion | flops 3145728 | bytes 12582960
  74.2 0.0 slice-done.2
  74.2 0.0 slice-done.3
  74.2 0.0 slice-start.1
  74.3 4.8 %bitcast_dynamic-update-slice_fusion.1 = bf16[512,48,5,128]{3,0,2,1:T(8,128)(2,1)} fusion(bf16[512,48,5,128]{3,0,2,1:T(8,128)(2,1)} %bitcast_dynamic-update-slice_fusion.2, bf16[48,512,128]{2,1,0:T(8,128)(2,1)S(1)} %bitcast.101, pred[48]{0:T(512)(128)(4,1)S(1)} %get-tuple-element.28), kind=kLoop, calls=%fused_computation.25 | loop fusion | flops 3145728 | bytes 12582960
  79.0 0.0 slice-done
  79.0 0.0 slice-done.1
  79.0 0.0 slice-start.5
  79.1 4.7 %bitcast_dynamic-update-slice_fusion = bf16[512,48,5,128]{3,0,2,1:T(8,128)(2,1)} fusion(bf16[512,48,5,128]{3,0,2,1:T(8,128)(2,1)} %bitcast_dynamic-update-slice_fusion.1, bf16[48,512,128]{2,1,0:T(8,128)(2,1)S(1)} %bitcast.99, pred[48]{0:T(512)(128)(4,1)S(1)} %get-tuple-element.15), kind=kLoop, calls=%fused_computation.24 | loop fusion | flops 3145728 | bytes 12582960
  83.7 0.0 slice-done.4
  83.7 0.0 slice-done.5
  83.7 4.7 %fusion.10 = bf16[512,48,5,128]{3,0,2,1:T(8,128)(2,1)} fusion(bf16[512,48,5,128]{3,0,2,1:T(8,128)(2,1)} %bitcast_dynamic-update-slice_fusion, bf16[48,512,128]{2,1,0:T(8,128)(2,1)S(1)} %bitcast.103, pred[48]{0:T(512)(128)(4,1)S(1)} %and_bitcast_fusion), kind=kLoop, calls=%fused_computation.23 | loop fusion | flops 3145728 | bytes 12582960 | tf_op jit(solution)/shard_map/stack | solution.py:50
  88.4 35.5 %all-gather.2.cloned.1.call-done = bf16[48,81920]{1,0:T(8,128)(2,1)} async-done(((bf16[48,5120]{1,0:T(8,128)(2,1)}), bf16[48,81920]{1,0:T(8,128)(2,1)}) %all-gather.2.cloned.1.call-update) | async-done | bytes 7864336 | tf_op jit(solution)/shard_map/all_gather | solution.py:32
  123.9 8.4 %copy.36 = bf16[6,8,640,128]{3,2,1,0:T(8,128)(2,1)} copy(bf16[6,8,640,128]{3,1,2,0:T(8,128)(2,1)} %bitcast.105) | data formatting | bytes 15728640
  132.3 26.4 %fusion.13 = (f32[48,128]{1,0:T(8,128)S(1)}, bf16[512,48,128]{0,2,1:T(8,128)(2,1)}, bf16[512,48,128]{0,2,1:T(8,128)(2,1)}) fusion(f32[512,48,128]{0,2,1:T(8,128)} %bitcast.104, f32[48,128]{1,0:T(8,128)S(1)} %bitcast_convert_fusion, bf16[512,48,5,128]{3,0,2,1:T(8,128)(2,1)} %fusion.10, bf16[48,5,128,128]{3,2,1,0:T(8,128)(2,1)} %bitcast.106), kind=kOutput, calls=%fused_computation.49 | convolution fusion | flops 4102023168 | bytes 64536576 | tf_op jit(solution)/shard_map/thkc,hkcd->thd/dot_general | solution.py:51
  158.7 21.6 %convolution_multiply_fusion = f32[48,5,128,128]{3,2,1,0:T(8,128)} fusion(bf16[512,48,5,128]{3,0,2,1:T(8,128)(2,1)} %fusion.10, bf16[512,48,128]{0,2,1:T(8,128)(2,1)} %get-tuple-element.14), kind=kOutput, calls=%fused_computation.20 | convolution fusion | flops 4030464000 | bytes 53477376 | tf_op jit(solution)/shard_map/thkc,thd->hkcd/dot_general | solution.py:58
  180.3 19.9 %copy.39 = f32[6,8,640,128]{3,1,2,0:T(8,128)} copy(f32[6,8,640,128]{3,2,1,0:T(8,128)} %bitcast.96) | data formatting | bytes 31457280
  200.2 0.0 reduce-scatter.2.cloned.1.call-update
  200.3 0.0 copy-start.1
  200.3 8.6 %copy.29 = bf16[512,6144]{1,0:T(8,128)(2,1)} copy(bf16[512,6144]{0,1:T(8,128)(2,1)} %bitcast.107) | data formatting | bytes 12582912
  208.9 60.9 %psum.15 = f32[6144]{0:T(1024)} all-reduce(f32[6144]{0:T(1024)S(1)} %multiply_bitcast_fusion), channel_id=1, replica_groups=mesh['row'=16,'col'=2] {'row'}, use_global_device_ids=true, to_apply=%region_3.5 | all-reduce | flops 6144 | bytes 49152 | tf_op jit(solution)/shard_map/psum | solution.py:64
  269.7 172.0 %reduce-scatter.2.cloned.1.call-done = f32[48,5120]{1,0:T(8,128)} async-done(((f32[48,81920]{1,0:T(8,128)}), f32[48,5120]{1,0:T(8,128)}) %reduce-scatter.2.cloned.1.call-update) | async-done | bytes 983056 | tf_op jit(solution)/shard_map/reduce_scatter | solution.py:62
  441.7 0.0 copy-done.1
  (16 shorter events, 0.1 us)
Async XLA Ops:
  8.0 11.5 %copy-start = (s32[96,5]{0,1:T(8,128)S(1)}, s32[96,5]{0,1:T(8,128)}, u32[]{:S(2)}) copy-start(s32[96,5]{0,1:T(8,128)} %param.10) | copy-start | bytes 5764
  8.0 43.9 %all-reduce.2.cloned.1.call-start = ((), (), s32[]{:S(2)}) async-start(), calls=%async_computation.1 | async-start | bytes 524288 | tf_op jit(solution)/shard_map/psum | solution.py:22
  14.6 109.3 %all-gather.2.cloned.1.call-start = ((), (), s32[]{:S(2)}) async-start(), calls=%async_computation.2 | async-start | bytes 8355840 | tf_op jit(solution)/shard_map/all_gather | solution.py:32
  15.2 426.5 %reduce-scatter.2.cloned.1.call-start = ((), (), s32[]{:S(2)}) async-start(), calls=%async_computation.3 | async-start | bytes 16711680 | tf_op jit(solution)/shard_map/reduce_scatter | solution.py:62
  15.2 42.6 %collective-permute-start = (bf16[512,3072]{0,1:T(8,128)(2,1)}, bf16[512,3072]{0,1:T(8,128)(2,1)}, u32[]{:S(2)}, u32[]{:S(2)}) collective-permute-start(bf16[512,3072]{0,1:T(8,128)(2,1)} %copy.17), channel_id=1, source_target_pairs={{1,0},{0,1},{3,2},{2,3},{5,4},{4,5},{7,6},{6,7},{9,8},{8,9},{11,10... | collective-permute-start | bytes 9437192 | tf_op jit(solution)/shard_map/ppermute | solution.py:17
  34.5 9.6 %copy-start.2 = (bf16[6144]{0:T(1024)(128)(2,1)S(1)}, bf16[6144]{0:T(1024)(128)(2,1)}, u32[]{:S(2)}) copy-start(bf16[6144]{0:T(1024)(128)(2,1)} %param.9) | copy-start | bytes 36868
  66.3 8.0 %slice-start.2 = ((s8[6291456]{0:T(1024)(128)(4,1)}), s8[4194304]{0:T(1024)(128)(4,1)S(1)}, s32[]{:S(2)}) async-start(s8[6291456]{0:T(1024)(128)(4,1)} %bitcast.100), calls=%async_computation.6 | async-start | bytes 8388608
  66.3 8.0 %slice-start.3 = ((s8[6291456]{0:T(1024)(128)(4,1)}), s8[2097152]{0:T(1024)(128)(4,1)S(1)}, s32[]{:S(2)}) async-start(s8[6291456]{0:T(1024)(128)(4,1)} %bitcast.100), calls=%async_computation.7 | async-start | bytes 4194304
  74.2 4.8 %slice-start = ((s8[6291456]{0:T(1024)(128)(4,1)}), s8[4194304]{0:T(1024)(128)(4,1)S(1)}, s32[]{:S(2)}) async-start(s8[6291456]{0:T(1024)(128)(4,1)} %bitcast.98), calls=%async_computation.4 | async-start | bytes 8388608
  74.2 4.8 %slice-start.1 = ((s8[6291456]{0:T(1024)(128)(4,1)}), s8[2097152]{0:T(1024)(128)(4,1)S(1)}, s32[]{:S(2)}) async-start(s8[6291456]{0:T(1024)(128)(4,1)} %bitcast.98), calls=%async_computation.5 | async-start | bytes 4194304
  79.0 4.7 %slice-start.4 = ((s8[6291456]{0:T(1024)(128)(4,1)}), s8[4194304]{0:T(1024)(128)(4,1)S(1)}, s32[]{:S(2)}) async-start(s8[6291456]{0:T(1024)(128)(4,1)} %bitcast.102), calls=%async_computation.8 | async-start | bytes 8388608
  79.0 4.7 %slice-start.5 = ((s8[6291456]{0:T(1024)(128)(4,1)}), s8[2097152]{0:T(1024)(128)(4,1)S(1)}, s32[]{:S(2)}) async-start(s8[6291456]{0:T(1024)(128)(4,1)} %bitcast.102), calls=%async_computation.9 | async-start | bytes 4194304
  200.3 241.5 %copy-start.1 = (s32[96,5]{0,1:T(8,128)S(1)}, s32[96,5]{0,1:T(8,128)}, u32[]{:S(2)}) copy-start(s32[96,5]{0,1:T(8,128)} %param.10) | copy-start | bytes 5764
Sparse Core Ops, SparseCore 0:
  14.7 20.0 all-reduce.1
Sparse Core Ops, SparseCore 1:
  17.8 106.0 all-gather.1
  200.3 241.3 reduce-scatter.1
where the time goes:
time: 452 us; the launch traced here: 449 us
  waiting for transfers between devices  208 us (46%)
  local copies, waits for them, and re-layouts  84.8 us (19%)
  blocking collectives  60.9 us (13%)
  matrix products  48 us (11%)
  other arithmetic  30.9 us (7%)
  between operations  15.6 us (3%)
    reduce_scatter x1, waiting for transfers between devices, body(): lax.psum_scatter(weight_terms, 'row', scatter_dimension=1, tiled=True)  172 us
    psum x1, blocking collectives, body(): bias_grad = lax.psum(bias_terms, 'row')  60.9 us
    unnamed x22, local copies, waits for them, and re-layouts  41.7 us
    all_gather x1, waiting for transfers between devices, body(): gathered_weights = lax.all_gather(w_blocks, 'row', axis=1, tiled=True)  35.5 us
    dot_general x1, matrix products, body(): jnp.einsum('thkc,hkcd->thd', picked, weights, preferred_element_type=jnp....  26.4 us
    unnamed x7, other arithmetic  25.2 us
    dot_general x1, matrix products, body(): jnp.einsum('thkc,thd->hkcd', picked, grad_rounded, preferred_element_type...  21.6 us
    gather x3, local copies, waits for them, and re-layouts, body(): jnp.take(source, my_pattern[:, level_index + 1] - home_panel * panel_bloc...  14.9 us
  transfers between devices with their start and end apart: 4, of which 2 were waited for; matrix products, arithmetic and copies ran while one was open for 18% of the time, Pallas kernels for 0%

commit v1 on v0

--- a/solution.py
+++ b/solution.py
@@ -1,14 +1,19 @@
+import functools
 import math
 
 import jax
 import jax.numpy as jnp
 from jax import lax
+from jax.experimental import pallas as pl
+from jax.experimental.pallas import tpu as pltpu
 from jax.sharding import PartitionSpec as P
 
 BLK = 128
 LEVELS = 3
 GLOB = 2
 KSLOT = 5
+MESH = pl.DeviceIdType.MESH
+VMEM_LIMIT = 60 * 1024 * 1024
 
 
 def from_behind(block, axis, distance):
@@ -22,7 +27,7 @@
     return lax.psum(kept, axis)
 
 
-def body(tokens, w_blocks, hidden_bias, pattern, grad_act):
+def plain_body(tokens, w_blocks, hidden_bias, pattern, grad_act):
     tok_rows = tokens.shape[0]
     local_blocks = w_blocks.shape[0]
     col_count = lax.axis_size("col")
@@ -65,6 +70,316 @@
     return (activation, weight_grad, bias_grad)
 
 
+def place(quads):
+    row = lax.axis_index("row")
+    return row, row // 4, (row // 2) % 2, row % 2, lax.axis_index("col")
+
+
+def greet(row, quad, bit_y, bit_x, col, quads, extra=()):
+    barrier = pltpu.get_barrier_semaphore()
+    peers = [(quad * 4 + bit_y * 2 + 1 - bit_x, col), (quad * 4 + (1 - bit_y) * 2 + bit_x, col)]
+    peers += [((quad + d) % quads * 4 + bit_y * 2 + bit_x, col) for d in range(1, quads)]
+    peers += list(extra)
+    for peer in peers:
+        pl.semaphore_signal(barrier, inc=1, device_id=peer, device_id_type=MESH)
+    pl.semaphore_wait(barrier, len(peers))
+
+
+def gather_kernel(quads, w_ref, tok_ref, all_ref, peer_ref,
+                  own_sem, tok_s, tok_r, z_s, z_r, y_s, y_r, x_s, x_r):
+    row, quad, bit_y, bit_x, col = place(quads)
+    half = w_ref.shape[0] // 2
+    x_peer = (quad * 4 + bit_y * 2 + 1 - bit_x, col)
+    y_peer = (quad * 4 + (1 - bit_y) * 2 + bit_x, col)
+    greet(row, quad, bit_y, bit_x, col, quads, [(row, 1 - col)])
+
+    def send(src, dst, s, r, peer):
+        copy = pltpu.make_async_remote_copy(
+            src_ref=src, dst_ref=dst, send_sem=s, recv_sem=r, device_id=peer, device_id_type=MESH
+        )
+        copy.start()
+        return copy
+
+    copies = []
+    own = pltpu.make_async_copy(w_ref, all_ref.at[row], own_sem)
+    own.start()
+    z_copies = []
+    for d in range(1, quads):
+        target = ((quad + d) % quads * 4 + bit_y * 2 + bit_x, col)
+        z_copies.append(send(w_ref, all_ref.at[row], z_s.at[d - 1], z_r.at[d - 1], target))
+    cut = [pl.ds(0, half), pl.ds(half, half)]
+    first_y, first_x = [], []
+    for d in range(quads):
+        src_row = (quad - d + quads) % quads * 4 + bit_y * 2 + bit_x
+        if d > 0:
+            z_copies[d - 1].wait_recv()
+        src = [w_ref.at[c] if d == 0 else all_ref.at[src_row, c] for c in cut]
+        dst = [all_ref.at[src_row, c] for c in cut]
+        first_y.append(send(src[0], dst[0], y_s.at[d], y_r.at[d], y_peer))
+        first_x.append(send(src[1], dst[1], x_s.at[d], x_r.at[d], x_peer))
+        copies.append(send(src[0], dst[0], x_s.at[quads + d], x_r.at[quads + d], x_peer))
+        copies.append(send(src[1], dst[1], y_s.at[quads + d], y_r.at[quads + d], y_peer))
+        if d == 0:
+            tok_copy = send(tok_ref, peer_ref, tok_s, tok_r, (row, 1 - col))
+    for d in range(quads):
+        from_quad = (quad - d + quads) % quads * 4
+        y_row = from_quad + (1 - bit_y) * 2 + bit_x
+        x_row = from_quad + bit_y * 2 + 1 - bit_x
+        first_y[d].wait_recv()
+        piece = all_ref.at[y_row, cut[0]]
+        copies.append(send(piece, piece, x_s.at[2 * quads + d], x_r.at[2 * quads + d], x_peer))
+        first_x[d].wait_recv()
+        piece = all_ref.at[x_row, cut[1]]
+        copies.append(send(piece, piece, y_s.at[2 * quads + d], y_r.at[2 * quads + d], y_peer))
+    for copy in copies:
+        copy.wait()
+    for copy in z_copies + first_y + first_x:
+        copy.wait_send()
+    tok_copy.wait()
+    own.wait()
+
+
+def gather(w_flat, tokens, quads):
+    any_spec = pl.BlockSpec(memory_space=pl.ANY)
+    dma = pltpu.SemaphoreType.DMA
+    return pl.pallas_call(
+        functools.partial(gather_kernel, quads),
+        out_shape=(
+            jax.ShapeDtypeStruct((quads * 4,) + w_flat.shape, w_flat.dtype),
+            jax.ShapeDtypeStruct(tokens.shape, tokens.dtype),
+        ),
+        in_specs=[pl.BlockSpec(memory_space=pltpu.VMEM), any_spec],
+        out_specs=(any_spec, any_spec),
+        scratch_shapes=[dma, dma, dma, dma((quads - 1,)), dma((quads - 1,)),
+                        dma((3 * quads,)), dma((3 * quads,)), dma((3 * quads,)), dma((3 * quads,))],
+        compiler_params=pltpu.CompilerParams(collective_id=0, has_side_effects=True,
+                                             vmem_limit_bytes=VMEM_LIMIT),
+    )(w_flat, tokens)
+
+
+def compute_kernel(rows, pairs_rows, scale, offsets, pat_ref, own_ref, peer_ref, shared_ref,
+                   w_ref, bias_ref, grad_ref, act_ref, part_ref, bgrad_ref):
+    step = pl.program_id(0)
+    weights = [w_ref[r].astype(jnp.float32) for r in range(rows)]
+    results = []
+    for j in range(2):
+        piece = pl.ds(j * BLK, BLK)
+        w = jnp.concatenate([v[j * pairs_rows:(j + 1) * pairs_rows] for v in weights], axis=0)
+        w = w.astype(jnp.bfloat16)
+        base = (2 * step + j) * KSLOT
+        picks = []
+        for k in range(KSLOT):
+            source = own_ref
+            if k == KSLOT - 1:
+                source = shared_ref
+            elif k > 0 and offsets[k - 1]:
+                source = peer_ref
+            at = pl.multiple_of(pat_ref[base + k] * BLK, BLK)
+            picks.append(source[:, pl.ds(at, BLK)])
+        sel = jnp.concatenate(picks, axis=1)
+        v = jnp.dot(sel, w, preferred_element_type=jnp.float32)
+        v = v + bias_ref[:, piece].astype(jnp.float32)
+        c = math.sqrt(2.0 / math.pi)
+        sq = v * v
+        t = jnp.tanh(v * (c + (c * 0.044715) * sq))
+        lift = 0.5 + 0.5 * t
+        act_ref[:, piece] = (v * lift).astype(jnp.bfloat16)
+        slope = lift + (0.5 * v) * (1.0 - t * t) * (c + (3.0 * 0.044715 * c) * sq)
+        grad = grad_ref[:, piece].astype(jnp.float32) * slope
+        bgrad_ref[:, piece] = jnp.sum(grad, axis=0, keepdims=True) * scale
+        out = lax.dot_general(sel, grad.astype(jnp.bfloat16), (((0,), (0,)), ((), ())),
+                              preferred_element_type=jnp.float32)
+        results.append(out * scale)
+    for r in range(rows):
+        cut = slice(r * pairs_rows, (r + 1) * pairs_rows)
+        part_ref[r] = jnp.concatenate([o[cut] for o in results], axis=0).astype(part_ref.dtype)
+
+
+def compute(pat, own, peer, shared, weights, bias, grad_act, rows, offsets, scale):
+    tok = own.shape[0]
+    hidden = grad_act.shape[1]
+    steps = hidden // (2 * BLK)
+    piece = weights.shape[1] // (2 * steps)
+    whole = lambda a: pl.BlockSpec(a.shape, lambda i, p: (0, 0))
+    wide = lambda n: pl.BlockSpec((n, 2 * BLK), lambda i, p: (0, i))
+    cube = pl.BlockSpec((rows, 2 * piece, BLK), lambda i, p: (0, i, 0))
+    return pl.pallas_call(
+        functools.partial(compute_kernel, rows, piece, scale, offsets),
+        out_shape=(
+            jax.ShapeDtypeStruct((tok, hidden), jnp.bfloat16),
+            jax.ShapeDtypeStruct(weights.shape, jnp.bfloat16),
+            jax.ShapeDtypeStruct((1, hidden), jnp.float32),
+        ),
+        grid_spec=pltpu.PrefetchScalarGridSpec(
+            num_scalar_prefetch=1, grid=(steps,),
+            in_specs=[whole(own), whole(peer), whole(shared), cube, wide(1), wide(tok)],
+            out_specs=[wide(tok), cube, wide(1)],
+        ),
+        compiler_params=pltpu.CompilerParams(vmem_limit_bytes=VMEM_LIMIT),
+    )(pat, own, peer, shared, weights, bias, grad_act)
+
+
+def scatter_kernel(quads, chunk, p_ref, b_ref, out_ref, bout_ref,
+                   first, second, second_out, third, third_out,
+                   bx, by, by_out, bz, bz_out,
+                   f_s, f_r, s_s, s_r, t_s, t_r, b_s, b_r):
+    row, quad, bit_y, bit_x, col = place(quads)
+    half = p_ref.shape[1] // 2
+    x_peer = (quad * 4 + bit_y * 2 + 1 - bit_x, col)
+    y_peer = (quad * 4 + (1 - bit_y) * 2 + bit_x, col)
+    peers = [x_peer, y_peer]
+    greet(row, quad, bit_y, bit_x, col, quads)
+
+    def send(src, dst, s, r, peer):
+        copy = pltpu.make_async_remote_copy(
+            src_ref=src, dst_ref=dst, send_sem=s, recv_sem=r, device_id=peer, device_id_type=MESH
+        )
+        copy.start()
+        return copy
+
+    def piece_row(quad_at, colour, near, far):
+        flip_x, flip_y = (near, far) if colour == 0 else (far, near)
+        x = (1 - bit_x) if flip_x else bit_x
+        y = (1 - bit_y) if flip_y else bit_y
+        return quad_at * 4 + y * 2 + x
+
+    order = list(range(1, quads)) + [0]
+    bias_copies = [send(b_ref, bx, b_s.at[0], b_r.at[0], x_peer)]
+    firsts = {}
+    for far in (1, 0):
+        for d in order:
+            at = (quad + d) % quads
+            for colour in range(2):
+                firsts[colour, far, d] = send(
+                    p_ref.at[piece_row(at, colour, 1, far), pl.ds(colour * half, half)],
+                    first.at[colour, far, d], f_s.at[colour, far, d], f_r.at[colour, far, d],
+                    peers[colour])
+    bias_copies[0].wait()
+    by_out[...] = b_ref[...] + bx[...]
+    bias_copies.append(send(by_out, by, b_s.at[1], b_r.at[1], y_peer))
+    seconds = {}
+    for d in order:
+        at = (quad + d) % quads
+        for colour in range(2):
+            firsts[colour, 1, d].wait_recv()
+            mine = piece_row(at, colour, 0, 1)
+
+            @pl.loop(0, half // chunk)
+            def _(i, colour=colour, d=d, mine=mine):
+                s = pl.multiple_of(i * chunk, chunk)
+                here = p_ref[mine, pl.ds(colour * half + s, chunk), :].astype(jnp.float32)
+                come = first[colour, 1, d, pl.ds(s, chunk), :].astype(jnp.float32)
+                second_out[colour, d, pl.ds(s, chunk), :] = (here + come).astype(jnp.bfloat16)
+
+            seconds[colour, d] = send(second_out.at[colour, d], second.at[colour, d],
+                                      s_s.at[colour, d], s_r.at[colour, d], peers[1 - colour])
+    bias_copies[1].wait()
+    bz_out[...] = by_out[...] + by[...]
+    for d in range(1, quads):
+        target = ((quad + d) % quads * 4 + bit_y * 2 + bit_x, col)
+        bias_copies.append(send(bz_out, bz.at[d - 1], b_s.at[d + 1], b_r.at[d + 1], target))
+    thirds = []
+    for d in order:
+        at = (quad + d) % quads
+        for colour in range(2):
+            firsts[colour, 0, d].wait_recv()
+            seconds[colour, d].wait_recv()
+            mine = piece_row(at, colour, 0, 0)
+
+            @pl.loop(0, half // chunk)
+            def _(i, colour=colour, d=d, mine=mine):
+                s = pl.multiple_of(i * chunk, chunk)
+                total = p_ref[mine, pl.ds(colour * half + s, chunk), :].astype(jnp.float32)
+                total += first[colour, 0, d, pl.ds(s, chunk), :].astype(jnp.float32)
+                total += second[colour, d, pl.ds(s, chunk), :].astype(jnp.float32)
+                if d == 0:
+                    out_ref[pl.ds(colour * half + s, chunk), :] = total
+                else:
+                    third_out[colour, d - 1, pl.ds(s, chunk), :] = total.astype(jnp.bfloat16)
+
+            if d > 0:
+                target = (at * 4 + bit_y * 2 + bit_x, col)
+                thirds.append(send(third_out.at[colour, d - 1], third.at[colour, d - 1],
+                                   t_s.at[colour, d - 1], t_r.at[colour, d - 1], target))
+    for copy in bias_copies[2:]:
+        copy.wait()
+    total = bz_out[...]
+    for d in range(quads - 1):
+        total += bz[d]
+    bout_ref[...] = total
+    for copy in thirds:
+        copy.wait()
+    for colour in range(2):
+        @pl.loop(0, half // chunk)
+        def _(i, colour=colour):
+            s = pl.multiple_of(i * chunk, chunk)
+            total = out_ref[pl.ds(colour * half + s, chunk), :]
+            for d in range(quads - 1):
+                total += third[colour, d, pl.ds(s, chunk), :].astype(jnp.float32)
+            out_ref[pl.ds(colour * half + s, chunk), :] = total
+    for copy in list(firsts.values()) + list(seconds.values()):
+        copy.wait_send()
+
+
+def scatter(parts, bias_terms, quads):
+    n = parts.shape[1]
+    half = n // 2
+    chunk = next(c for c in (192, 160, 128, 96, 80, 64, 48, 32, 16) if half % c == 0)
+    vmem = pl.BlockSpec(memory_space=pltpu.VMEM)
+    dma = pltpu.SemaphoreType.DMA
+    bf = lambda *s: pltpu.VMEM(s, jnp.bfloat16)
+    f32 = lambda *s: pltpu.VMEM(s, jnp.float32)
+    b = bias_terms.shape
+    return pl.pallas_call(
+        functools.partial(scatter_kernel, quads, chunk),
+        out_shape=(jax.ShapeDtypeStruct((n, BLK), jnp.float32),
+                   jax.ShapeDtypeStruct(b, jnp.float32)),
+        in_specs=[vmem, vmem],
+        out_specs=(vmem, vmem),
+        scratch_shapes=[
+            bf(2, 2, quads, half, BLK), bf(2, quads, half, BLK), bf(2, quads, half, BLK),
+            bf(2, quads - 1, half, BLK), bf(2, quads - 1, half, BLK),
+            f32(*b), f32(*b), f32(*b), f32(quads - 1, *b), f32(*b),
+            dma((2, 2, quads)), dma((2, 2, quads)), dma((2, quads)), dma((2, quads)),
+            dma((2, quads - 1)), dma((2, quads - 1)), dma((quads + 1,)), dma((quads + 1,)),
+        ],
+        compiler_params=pltpu.CompilerParams(collective_id=1, has_side_effects=True,
+                                             vmem_limit_bytes=VMEM_LIMIT),
+    )(parts, bias_terms)
+
+
+def kernel_body(tokens, w_blocks, hidden_bias, pattern, grad_act):
+    tok_rows = tokens.shape[0]
+    local_blocks, width = w_blocks.shape
+    rows = lax.axis_size("row")
+    quads = rows // 4
+    col_count = lax.axis_size("col")
+    col = lax.axis_index("col")
+    panel_blocks = tokens.shape[1] // BLK
+    scale = 1.0 / math.sqrt(tok_rows * rows)
+    offsets = [2**level % col_count for level in range(LEVELS)]
+    mine = lax.dynamic_slice_in_dim(pattern, col * local_blocks, local_blocks, 0)
+    homes = [(col + o) % col_count * panel_blocks for o in [0] + offsets] + [0]
+    pat = (mine - jnp.stack([jnp.asarray(h, jnp.int32) for h in homes])).reshape(-1)
+    flat = w_blocks.reshape(local_blocks * width // BLK, BLK)
+    weights, peer = gather(flat, tokens, quads)
+    shared = jnp.where(col == 0, tokens[:, : GLOB * BLK], peer[:, : GLOB * BLK])
+    activation, parts, bias_terms = compute(
+        pat, tokens, peer, shared, weights, hidden_bias.reshape(1, -1), grad_act,
+        rows, offsets, scale)
+    weight_grad, bias_grad = scatter(parts, bias_terms.reshape(-1, BLK), quads)
+    return activation, weight_grad.reshape(local_blocks, width), bias_grad.reshape(-1)
+
+
+def body(tokens, w_blocks, hidden_bias, pattern, grad_act):
+    rows = lax.axis_size("row")
+    piece = w_blocks.shape[1] // BLK
+    fits = lax.axis_size("col") == 2 and rows % 4 == 0 and rows > 4
+    fits = fits and piece % 8 == 0 and w_blocks.shape[0] % 4 == 0
+    run = kernel_body if fits else plain_body
+    return run(tokens, w_blocks, hidden_bias, pattern, grad_act)
+
+
 def solution(mesh):
     return jax.shard_map(
         body,

time: 452 us -> 240 us (0.53)
  Pallas kernels: 0 us -> 228 us
  waiting for transfers between devices: 208 us -> 0 us
  local copies, waits for them, and re-layouts: 84.8 us -> 7.85 us
  blocking collectives: 60.9 us -> 0 us
  matrix products: 48 us -> 0 us
  other arithmetic: 30.9 us -> 2.53 us
  between operations: 15.6 us -> 0.67 us
    pallas_call x0 -> x3, Pallas kernels: none -> 228 us  [the longest x1 110 us: scatter(): pl.pallas_call(functools.partial(scatter_kernel, quads, chunk), out_shape...]
    reduce_scatter x1 -> x0, waiting for transfers between devices: 172 us -> none  [body(): lax.psum_scatter(weight_terms, 'row', scatter_dimension=1, tiled=True)]
    psum x1 -> x0, blocking collectives: 60.9 us -> none  [body(): bias_grad = lax.psum(bias_terms, 'row')]
    dot_general x2 -> x0, matrix products: 48 us -> none  [the longest x1 26.4 us: body(): jnp.einsum('thkc,hkcd->thd', picked, weights, preferred_element_type=jnp....]
    unnamed x22 -> x1, local copies, waits for them, and re-layouts: 41.7 us -> 1.35 us
    all_gather x1 -> x0, waiting for transfers between devices: 35.5 us -> none  [body(): gathered_weights = lax.all_gather(w_blocks, 'row', axis=1, tiled=True)]
    gather x5 -> x0, local copies, waits for them, and re-layouts: 25.8 us -> none  [the longest x3 14.9 us: body(): jnp.take(source, my_pattern[:, level_index + 1] - home_panel * panel_bloc...]
    unnamed x7 -> x0, other arithmetic: 25.2 us -> none
  transfers between devices with their start and end apart: 4 -> 0, of which waited for: 2 -> 0; matrix products, arithmetic and copies ran while one was open for 18% -> 0% of each run, Pallas kernels for 0% -> 0%
where the time goes in v1:
time: 240 us; the launch traced here: 239 us
  Pallas kernels  228 us (95%)
  local copies, waits for them, and re-layouts  7.85 us (3%)
  other arithmetic  2.53 us (1%)
    pallas_call x1, Pallas kernels, scatter(): pl.pallas_call(functools.partial(scatter_kernel, quads, chunk), out_shape...  110 us
    pallas_call x1, Pallas kernels, gather(): pl.pallas_call(functools.partial(gather_kernel, quads), out_shape=(jax.Sh...  79.4 us
    pallas_call x1, Pallas kernels, compute(): pl.pallas_call(functools.partial(compute_kernel, rows, piece, scale, offs...  38.9 us

profile of v1, /device:TPU:9, one launch (start us, length us, event | category | flops | bytes accessed | tf_op | source)
XLA Modules:
  0.0 239.4 jit_solution(829122027787384364)
XLA Ops:
  0.7 0.1 stack.13
  0.7 0.8 dynamic-slice_subtract_fusion
  1.5 0.1 copy.8
  1.6 0.7 reshape.25.pat_ref
  2.3 1.3 reshape.27.bias_ref
  3.6 2.0 reshape.26.w_ref
  5.6 79.4 %shard_map.76 = (bf16[16,1920,128]{2,1,0:T(8,128)(2,1)}, bf16[512,3072]{1,0:T(8,128)(2,1)}) custom-call(bf16[1920,128]{1,0:T(8,128)(2,1)} %reshape.26.w_ref, bf16[512,3072]{1,0:T(8,128)(2,1)} %own_ref.1), custom_call_target="tpu_custom_call" | custom-call | tf_op jit(solution)/shard_map/pallas_call | solution.py:145
  85.1 1.8 slice_select_fusion.shared_ref
  86.9 38.9 %shard_map.77 = (bf16[512,6144]{1,0:T(8,128)(2,1)}, bf16[16,1920,128]{2,1,0:T(8,128)(2,1)}, f32[1,6144]{1,0:T(1,128)}) custom-call(s32[240]{0:T(256)} %reshape.25.pat_ref, bf16[512,3072]{1,0:T(8,128)(2,1)} %own_ref.1, bf16[512,3072]{1,0:T(8,128)(2,1)} %get-tuple-element.10.peer_ref, bf16[512,256]{1,0:T(8,128)(2,1)} %slice_select_fusion.shared_ref, ...), custom_call_target="tpu_custom_call" | custom-call | tf_op jit(solution)/shard_map/pallas_call | solution.py:206
  125.8 109.9 %shard_map.78 = (f32[1920,128]{1,0:T(8,128)}, f32[48,128]{1,0:T(8,128)}) custom-call(bf16[16,1920,128]{2,1,0:T(8,128)(2,1)} %get-tuple-element.13.p_ref, f32[48,128]{1,0:T(8,128)} %bitcast.4), custom_call_target="tpu_custom_call" | custom-call | tf_op jit(solution)/shard_map/pallas_call | solution.py:333
  235.7 2.3 reshape.29
  238.0 1.3 copy.10

commit v2 on v0

--- a/solution.py
+++ b/solution.py
@@ -1,14 +1,19 @@
+import functools
 import math
 
 import jax
 import jax.numpy as jnp
 from jax import lax
+from jax.experimental import pallas as pl
+from jax.experimental.pallas import tpu as pltpu
 from jax.sharding import PartitionSpec as P
 
 BLK = 128
 LEVELS = 3
 GLOB = 2
 KSLOT = 5
+MESH = pl.DeviceIdType.MESH
+VMEM_LIMIT = 60 * 1024 * 1024
 
 
 def from_behind(block, axis, distance):
@@ -22,7 +27,7 @@
     return lax.psum(kept, axis)
 
 
-def body(tokens, w_blocks, hidden_bias, pattern, grad_act):
+def plain_body(tokens, w_blocks, hidden_bias, pattern, grad_act):
     tok_rows = tokens.shape[0]
     local_blocks = w_blocks.shape[0]
     col_count = lax.axis_size("col")
@@ -65,6 +70,338 @@
     return (activation, weight_grad, bias_grad)
 
 
+def place(quads):
+    row = lax.axis_index("row")
+    return row, row // 4, (row // 2) % 2, row % 2, lax.axis_index("col")
+
+
+def greet(row, quad, bit_y, bit_x, col, quads, extra=()):
+    barrier = pltpu.get_barrier_semaphore()
+    peers = [(quad * 4 + bit_y * 2 + 1 - bit_x, col), (quad * 4 + (1 - bit_y) * 2 + bit_x, col)]
+    peers += [((quad + d) % quads * 4 + bit_y * 2 + bit_x, col) for d in range(1, quads)]
+    peers += list(extra)
+    for peer in peers:
+        pl.semaphore_signal(barrier, inc=1, device_id=peer, device_id_type=MESH)
+    pl.semaphore_wait(barrier, len(peers))
+
+
+def gather_kernel(quads, w_ref, tok_ref, all_ref, peer_ref,
+                  own_sem, tok_s, tok_r, z_s, z_r, y_s, y_r, x_s, x_r):
+    row, quad, bit_y, bit_x, col = place(quads)
+    half = w_ref.shape[0] // 2
+    x_peer = (quad * 4 + bit_y * 2 + 1 - bit_x, col)
+    y_peer = (quad * 4 + (1 - bit_y) * 2 + bit_x, col)
+    greet(row, quad, bit_y, bit_x, col, quads, [(row, 1 - col)])
+
+    def send(src, dst, s, r, peer):
+        copy = pltpu.make_async_remote_copy(
+            src_ref=src, dst_ref=dst, send_sem=s, recv_sem=r, device_id=peer, device_id_type=MESH
+        )
+        copy.start()
+        return copy
+
+    copies = []
+    own = pltpu.make_async_copy(w_ref, all_ref.at[row], own_sem)
+    own.start()
+    z_copies = []
+    for d in range(1, quads):
+        target = ((quad + d) % quads * 4 + bit_y * 2 + bit_x, col)
+        z_copies.append(send(w_ref, all_ref.at[row], z_s.at[d - 1], z_r.at[d - 1], target))
+    cut = [pl.ds(0, half), pl.ds(half, half)]
+    first_y, first_x = [], []
+    for d in range(quads):
+        src_row = (quad - d + quads) % quads * 4 + bit_y * 2 + bit_x
+        if d > 0:
+            z_copies[d - 1].wait_recv()
+        src = [w_ref.at[c] if d == 0 else all_ref.at[src_row, c] for c in cut]
+        dst = [all_ref.at[src_row, c] for c in cut]
+        first_y.append(send(src[0], dst[0], y_s.at[d], y_r.at[d], y_peer))
+        first_x.append(send(src[1], dst[1], x_s.at[d], x_r.at[d], x_peer))
+        copies.append(send(src[0], dst[0], x_s.at[quads + d], x_r.at[quads + d], x_peer))
+        copies.append(send(src[1], dst[1], y_s.at[quads + d], y_r.at[quads + d], y_peer))
+        if d == 0:
+            tok_copy = send(tok_ref, peer_ref, tok_s, tok_r, (row, 1 - col))
+    for d in range(quads):
+        from_quad = (quad - d + quads) % quads * 4
+        y_row = from_quad + (1 - bit_y) * 2 + bit_x
+        x_row = from_quad + bit_y * 2 + 1 - bit_x
+        first_y[d].wait_recv()
+        piece = all_ref.at[y_row, cut[0]]
+        copies.append(send(piece, piece, x_s.at[2 * quads + d], x_r.at[2 * quads + d], x_peer))
+        first_x[d].wait_recv()
+        piece = all_ref.at[x_row, cut[1]]
+        copies.append(send(piece, piece, y_s.at[2 * quads + d], y_r.at[2 * quads + d], y_peer))
+    for copy in copies:
+        copy.wait()
+    for copy in z_copies + first_y + first_x:
+        copy.wait_send()
+    tok_copy.wait()
+    own.wait()
+
+
+def gather(w_flat, tokens, quads):
+    any_spec = pl.BlockSpec(memory_space=pl.ANY)
+    dma = pltpu.SemaphoreType.DMA
+    return pl.pallas_call(
+        functools.partial(gather_kernel, quads),
+        out_shape=(
+            jax.ShapeDtypeStruct((quads * 4,) + w_flat.shape, w_flat.dtype),
+            jax.ShapeDtypeStruct(tokens.shape, tokens.dtype),
+        ),
+        in_specs=[pl.BlockSpec(memory_space=pltpu.VMEM), any_spec],
+        out_specs=(any_spec, any_spec),
+        scratch_shapes=[dma, dma, dma, dma((quads - 1,)), dma((quads - 1,)),
+                        dma((3 * quads,)), dma((3 * quads,)), dma((3 * quads,)), dma((3 * quads,))],
+        compiler_params=pltpu.CompilerParams(collective_id=0, has_side_effects=True,
+                                             vmem_limit_bytes=VMEM_LIMIT),
+    )(w_flat, tokens)
+
+
+def fused_kernel(quads, chunks, blk_rows, strip, scale,
+                 pat_ref, own_ref, peer_ref, w_ref, bias_ref, grad_ref,
+                 act_ref, out_ref, bout_ref,
+                 table, p_ref, b_ref, first, second, second_out, third, third_out,
+                 bx, by, by_out, bz, bz_out,
+                 f_s, f_r, s_s, s_r, t_s, t_r, b_s, b_r):
+    step = pl.program_id(0)
+    steps = pl.num_programs(0)
+    rows = quads * 4
+    row, quad, bit_y, bit_x, col = place(quads)
+    n = first.shape[3]
+    half = p_ref.shape[1] // 2
+    per = p_ref.shape[1] // chunks // (2 * blk_rows)
+    peers = [(quad * 4 + bit_y * 2 + 1 - bit_x, col), (quad * 4 + (1 - bit_y) * 2 + bit_x, col)]
+
+    @pl.when(step == 0)
+    def _():
+        greet(row, quad, bit_y, bit_x, col, quads)
+
+        panel = own_ref.shape[1] // BLK
+        for i in range(panel):
+            table[col * panel + i] = own_ref[:, i * BLK:(i + 1) * BLK]
+            table[(1 - col) * panel + i] = peer_ref[:, i * BLK:(i + 1) * BLK]
+
+    pair = pair_of(step, per, chunks)
+    weights = [w_ref[r].astype(jnp.float32) for r in range(rows)]
+    results = []
+    for j in range(2):
+        piece = pl.ds(j * BLK, BLK)
+        w = jnp.concatenate([v[j * blk_rows:(j + 1) * blk_rows] for v in weights], axis=0)
+        w = w.astype(jnp.bfloat16)
+        base = (2 * pair + j) * KSLOT
+        picks = [table[pat_ref[base + k]] for k in range(KSLOT)]
+        sel = jnp.concatenate(picks, axis=1)
+        v = jnp.dot(sel, w, preferred_element_type=jnp.float32)
+        v = v + bias_ref[:, piece].astype(jnp.float32)
+        c = math.sqrt(2.0 / math.pi)
+        sq = v * v
+        t = jnp.tanh(v * (c + (c * 0.044715) * sq))
+        lift = 0.5 + 0.5 * t
+        act_ref[:, piece] = (v * lift).astype(jnp.bfloat16)
+        slope = lift + (0.5 * v) * (1.0 - t * t) * (c + (3.0 * 0.044715 * c) * sq)
+        grad = grad_ref[:, piece].astype(jnp.float32) * slope
+        b_ref[pl.ds(2 * pair + j, 1), :] = jnp.sum(grad, axis=0, keepdims=True) * scale
+        out = lax.dot_general(sel, grad.astype(jnp.bfloat16), (((0,), (0,)), ((), ())),
+                              preferred_element_type=jnp.float32)
+        results.append(out * scale)
+    at = pl.multiple_of(pair * (2 * blk_rows), 2 * blk_rows)
+    for r in range(rows):
+        cut = slice(r * blk_rows, (r + 1) * blk_rows)
+        p_ref[r, pl.ds(at, 2 * blk_rows), :] = jnp.concatenate(
+            [o[cut] for o in results], axis=0).astype(p_ref.dtype)
+
+    def link(src, dst, s, r, peer):
+        return pltpu.make_async_remote_copy(
+            src_ref=src, dst_ref=dst, send_sem=s, recv_sem=r, device_id=peer, device_id_type=MESH
+        )
+
+    def piece_row(d, colour, near, far):
+        flip_x, flip_y = (near, far) if colour == 0 else (far, near)
+        x = (1 - bit_x) if flip_x else bit_x
+        y = (1 - bit_y) if flip_y else bit_y
+        return (quad + d) % quads * 4 + y * 2 + x
+
+    order = list(range(1, quads)) + [0]
+    start = lambda c: (c % 2) * half + (c // 2) * n
+
+    def first_copy(c, far, d):
+        return link(p_ref.at[piece_row(d, c % 2, 1, far), pl.ds(start(c), n)],
+                    first.at[c, far, d], f_s.at[c, far, d], f_r.at[c, far, d], peers[c % 2])
+
+    def second_copy(c, d):
+        return link(second_out.at[c, d], second.at[c, d], s_s.at[c, d], s_r.at[c, d],
+                    peers[1 - c % 2])
+
+    def third_copy(c, d):
+        target = ((quad + d) % quads * 4 + bit_y * 2 + bit_x, col)
+        return link(third_out.at[c, d - 1], third.at[c, d - 1],
+                    t_s.at[c, d - 1], t_r.at[c, d - 1], target)
+
+    def do_first(c):
+        for far in (1, 0):
+            for d in order:
+                first_copy(c, far, d).start()
+
+    def do_second(c):
+        for d in order:
+            first_copy(c, 1, d).wait_recv()
+            mine = piece_row(d, c % 2, 0, 1)
+
+            @pl.loop(0, n // strip)
+            def _(i, d=d, mine=mine):
+                s = pl.multiple_of(i * strip, strip)
+                here = p_ref[mine, pl.ds(start(c) + s, strip), :].astype(jnp.float32)
+                come = first[c, 1, d, pl.ds(s, strip), :].astype(jnp.float32)
+                second_out[c, d, pl.ds(s, strip), :] = (here + come).astype(jnp.bfloat16)
+
+            second_copy(c, d).start()
+
+    def do_third(c):
+        for d in order:
+            first_copy(c, 0, d).wait_recv()
+            second_copy(c, d).wait_recv()
+            mine = piece_row(d, c % 2, 0, 0)
+
+            @pl.loop(0, n // strip)
+            def _(i, d=d, mine=mine):
+                s = pl.multiple_of(i * strip, strip)
+                total = p_ref[mine, pl.ds(start(c) + s, strip), :].astype(jnp.float32)
+                total += first[c, 0, d, pl.ds(s, strip), :].astype(jnp.float32)
+                total += second[c, d, pl.ds(s, strip), :].astype(jnp.float32)
+                if d == 0:
+                    out_ref[pl.ds(start(c) + s, strip), :] = total
+                else:
+                    third_out[c, d - 1, pl.ds(s, strip), :] = total.astype(jnp.bfloat16)
+
+            if d > 0:
+                third_copy(c, d).start()
+
+    for c in range(chunks):
+        @pl.when(step == (c + 1) * per - 1)
+        def _(c=c):
+            do_first(c)
+            if c >= 2 and c < chunks - 1:
+                do_second(c - 2)
+
+    @pl.when(step == steps - 1)
+    def _():
+        to_x = link(b_ref, bx, b_s.at[0], b_r.at[0], peers[0])
+        to_x.start()
+        do_second(chunks - 3)
+        do_second(chunks - 2)
+        to_x.wait()
+        by_out[...] = b_ref[...] + bx[...]
+        to_y = link(by_out, by, b_s.at[1], b_r.at[1], peers[1])
+        to_y.start()
+        do_third(0)
+        do_second(chunks - 1)
+        to_y.wait()
+        bz_out[...] = by_out[...] + by[...]
+        to_z = []
+        for d in range(1, quads):
+            target = ((quad + d) % quads * 4 + bit_y * 2 + bit_x, col)
+            to_z.append(link(bz_out, bz.at[d - 1], b_s.at[d + 1], b_r.at[d + 1], target))
+            to_z[-1].start()
+        for c in range(1, chunks):
+            do_third(c)
+        for copy in to_z:
+            copy.wait()
+        total = bz_out[...]
+        for d in range(quads - 1):
+            total += bz[d]
+        bout_ref[...] = total
+        for c in range(chunks):
+            for d in range(1, quads):
+                third_copy(c, d).wait()
+
+            @pl.loop(0, n // strip)
+            def _(i, c=c):
+                s = pl.multiple_of(i * strip, strip)
+                total = out_ref[pl.ds(start(c) + s, strip), :]
+                for d in range(quads - 1):
+                    total += third[c, d, pl.ds(s, strip), :].astype(jnp.float32)
+                out_ref[pl.ds(start(c) + s, strip), :] = total
+        for c in range(chunks):
+            for d in order:
+                first_copy(c, 0, d).wait_send()
+                first_copy(c, 1, d).wait_send()
+                second_copy(c, d).wait_send()
+
+
+def pair_of(step, per, chunks):
+    chunk = step // per
+    return (chunk % 2) * (per * chunks // 2) + (chunk // 2) * per + step % per
+
+
+def fused(pat, own, peer, weights, bias, grad_act, quads, scale):
+    tok, hidden = grad_act.shape
+    blocks = hidden // BLK
+    steps = blocks // 2
+    chunks = 4
+    per = steps // chunks
+    total_rows = weights.shape[1]
+    blk_rows = total_rows // blocks
+    n = total_rows // chunks
+    strip = next(c for c in (160, 128, 96, 80, 64, 48, 32, 16) if n % c == 0)
+    rows = quads * 4
+    whole = lambda a: pl.BlockSpec(a.shape, lambda i, p: (0, 0))
+    wide = lambda m: pl.BlockSpec((m, 2 * BLK), lambda i, p: (0, pair_of(i, per, chunks)))
+    fixed = lambda *s: pl.BlockSpec(s, lambda i, p: (0, 0))
+    cube = pl.BlockSpec((rows, 2 * blk_rows, BLK), lambda i, p: (0, pair_of(i, per, chunks), 0))
+    dma = pltpu.SemaphoreType.DMA
+    bf = lambda *s: pltpu.VMEM(s, jnp.bfloat16)
+    f32 = lambda *s: pltpu.VMEM(s, jnp.float32)
+    b = (blocks, BLK)
+    return pl.pallas_call(
+        functools.partial(fused_kernel, quads, chunks, blk_rows, strip, scale),
+        out_shape=(
+            jax.ShapeDtypeStruct((tok, hidden), jnp.bfloat16),
+            jax.ShapeDtypeStruct((total_rows, BLK), jnp.float32),
+            jax.ShapeDtypeStruct(b, jnp.float32),
+        ),
+        grid_spec=pltpu.PrefetchScalarGridSpec(
+            num_scalar_prefetch=1, grid=(steps,),
+            in_specs=[whole(own), whole(peer), cube, wide(1), wide(tok)],
+            out_specs=[wide(tok), fixed(total_rows, BLK), fixed(*b)],
+            scratch_shapes=[
+                bf(2 * own.shape[1] // BLK, tok, BLK), bf(rows, total_rows, BLK), f32(*b),
+                bf(chunks, 2, quads, n, BLK), bf(chunks, quads, n, BLK), bf(chunks, quads, n, BLK),
+                bf(chunks, quads - 1, n, BLK), bf(chunks, quads - 1, n, BLK),
+                f32(*b), f32(*b), f32(*b), f32(quads - 1, *b), f32(*b),
+                dma((chunks, 2, quads)), dma((chunks, 2, quads)), dma((chunks, quads)),
+                dma((chunks, quads)), dma((chunks, quads - 1)), dma((chunks, quads - 1)),
+                dma((quads + 1,)), dma((quads + 1,)),
+            ],
+        ),
+        compiler_params=pltpu.CompilerParams(collective_id=1, has_side_effects=True,
+                                             vmem_limit_bytes=VMEM_LIMIT),
+    )(pat, own, peer, weights, bias, grad_act)
+
+
+def kernel_body(tokens, w_blocks, hidden_bias, pattern, grad_act):
+    tok_rows = tokens.shape[0]
+    local_blocks, width = w_blocks.shape
+    rows = lax.axis_size("row")
+    quads = rows // 4
+    col = lax.axis_index("col")
+    scale = 1.0 / math.sqrt(tok_rows * rows)
+    pat = lax.dynamic_slice_in_dim(pattern, col * local_blocks, local_blocks, 0).reshape(-1)
+    flat = w_blocks.reshape(local_blocks * width // BLK, BLK)
+    weights, peer = gather(flat, tokens, quads)
+    activation, weight_grad, bias_grad = fused(
+        pat, tokens, peer, weights, hidden_bias.reshape(1, -1), grad_act, quads, scale)
+    return activation, weight_grad.reshape(local_blocks, width), bias_grad.reshape(-1)
+
+
+def body(tokens, w_blocks, hidden_bias, pattern, grad_act):
+    rows = lax.axis_size("row")
+    piece = w_blocks.shape[1] // BLK
+    fits = lax.axis_size("col") == 2 and rows % 4 == 0 and rows > 4
+    fits = fits and piece % 8 == 0 and w_blocks.shape[0] % 8 == 0
+    run = kernel_body if fits else plain_body
+    return run(tokens, w_blocks, hidden_bias, pattern, grad_act)
+
+
 def solution(mesh):
     return jax.shard_map(
         body,

time: 452 us -> 231 us (0.51)
  Pallas kernels: 0 us -> 216 us
  waiting for transfers between devices: 208 us -> 0 us
  local copies, waits for them, and re-layouts: 84.8 us -> 14 us
  blocking collectives: 60.9 us -> 0 us
  matrix products: 48 us -> 0 us
  other arithmetic: 30.9 us -> 0 us
  between operations: 15.6 us -> 0.66 us
    pallas_call x0 -> x2, Pallas kernels: none -> 216 us  [the longest x1 136 us: fused(): pl.pallas_call(functools.partial(fused_kernel, quads, chunks, blk_rows, s...]
    reduce_scatter x1 -> x0, waiting for transfers between devices: 172 us -> none  [body(): lax.psum_scatter(weight_terms, 'row', scatter_dimension=1, tiled=True)]
    psum x1 -> x0, blocking collectives: 60.9 us -> none  [body(): bias_grad = lax.psum(bias_terms, 'row')]
    dot_general x2 -> x0, matrix products: 48 us -> none  [the longest x1 26.4 us: body(): jnp.einsum('thkc,hkcd->thd', picked, weights, preferred_element_type=jnp....]
    all_gather x1 -> x0, waiting for transfers between devices: 35.5 us -> none  [body(): gathered_weights = lax.all_gather(w_blocks, 'row', axis=1, tiled=True)]
    unnamed x22 -> x6, local copies, waits for them, and re-layouts: 41.7 us -> 7.53 us
    gather x5 -> x0, local copies, waits for them, and re-layouts: 25.8 us -> none  [the longest x3 14.9 us: body(): jnp.take(source, my_pattern[:, level_index + 1] - home_panel * panel_bloc...]
    unnamed x7 -> x0, other arithmetic: 25.2 us -> none
  transfers between devices with their start and end apart: 4 -> 0, of which waited for: 2 -> 0; matrix products, arithmetic and copies ran while one was open for 18% -> 0% of each run, Pallas kernels for 0% -> 0%
where the time goes in v2:
time: 231 us; the launch traced here: 230 us
  Pallas kernels  216 us (94%)
  local copies, waits for them, and re-layouts  14 us (6%)
    pallas_call x1, Pallas kernels, fused(): pl.pallas_call(functools.partial(fused_kernel, quads, chunks, blk_rows, s...  136 us
    pallas_call x1, Pallas kernels, gather(): pl.pallas_call(functools.partial(gather_kernel, quads), out_shape=(jax.Sh...  79.4 us
    unnamed x6, local copies, waits for them, and re-layouts  7.53 us

profile of v2, /device:TPU:9, one launch (start us, length us, event | category | flops | bytes accessed | tf_op | source)
XLA Modules:
  0.0 230.5 jit_solution(3123640551339406779)
XLA Ops:
  0.6 0.0 copy-start
  0.6 0.7 copy-done
  1.3 0.1 constant_dynamic-slice_fusion
  1.4 0.1 copy.8
  1.5 0.7 reshape.21.pat_ref
  2.2 1.3 reshape.23.bias_ref
  3.5 2.0 reshape.22.w_ref
  5.5 79.4 %shard_map.76 = (bf16[16,1920,128]{2,1,0:T(8,128)(2,1)}, bf16[512,3072]{1,0:T(8,128)(2,1)}) custom-call(bf16[1920,128]{1,0:T(8,128)(2,1)} %reshape.22.w_ref, bf16[512,3072]{1,0:T(8,128)(2,1)} %own_ref.1), custom_call_target="tpu_custom_call" | custom-call | tf_op jit(solution)/shard_map/pallas_call | solution.py:145
  85.0 136.3 %shard_map.77 = (bf16[512,6144]{1,0:T(8,128)(2,1)}, f32[1920,128]{1,0:T(8,128)}, f32[48,128]{1,0:T(8,128)}) custom-call(s32[240]{0:T(256)} %reshape.21.pat_ref, bf16[512,3072]{1,0:T(8,128)(2,1)} %own_ref.1, bf16[512,3072]{1,0:T(8,128)(2,1)} %get-tuple-element.8.peer_ref, bf16[16,1920,128]{2,1,0:T(8,128)(2,1)} %get-tuple-element.9.w_ref, ...), custom_call_target="tpu_custom_call" | custom-call | tf_op jit(solution)/shard_map/pallas_call | solution.py:355
  221.3 2.3 reshape.24
  223.6 0.0 copy-start.1
  223.6 6.2 %copy.11 = bf16[512,6144]{1,0:T(8,128)(2,1)} copy(bf16[512,6144]{1,0:T(8,128)(2,1)} %get-tuple-element.16) | data formatting | bytes 12582912
  229.9 0.0 copy-done.1
  229.9 0.6 copy.12
Async XLA Ops:
  0.6 0.7 copy-start
  223.6 6.2 %copy-start.1 = (f32[48,128]{1,0:T(8,128)S(1)}, f32[48,128]{1,0:T(8,128)}, u32[]{:S(2)}) copy-start(f32[48,128]{1,0:T(8,128)} %get-tuple-element.12) | copy-start | bytes 73732

commit v3 on v2

--- a/solution.py
+++ b/solution.py
@@ -280,21 +280,23 @@
         @pl.when(step == (c + 1) * per - 1)
         def _(c=c):
             do_first(c)
-            if c >= 2 and c < chunks - 1:
+            if c >= 2:
                 do_second(c - 2)
+            if c >= 4:
+                do_third(c - 4)
 
     @pl.when(step == steps - 1)
     def _():
         to_x = link(b_ref, bx, b_s.at[0], b_r.at[0], peers[0])
         to_x.start()
-        do_second(chunks - 3)
         do_second(chunks - 2)
+        do_third(chunks - 4)
         to_x.wait()
         by_out[...] = b_ref[...] + bx[...]
         to_y = link(by_out, by, b_s.at[1], b_r.at[1], peers[1])
         to_y.start()
-        do_third(0)
         do_second(chunks - 1)
+        do_third(chunks - 3)
         to_y.wait()
         bz_out[...] = by_out[...] + by[...]
         to_z = []
@@ -302,8 +304,8 @@
             target = ((quad + d) % quads * 4 + bit_y * 2 + bit_x, col)
             to_z.append(link(bz_out, bz.at[d - 1], b_s.at[d + 1], b_r.at[d + 1], target))
             to_z[-1].start()
-        for c in range(1, chunks):
-            do_third(c)
+        do_third(chunks - 2)
+        do_third(chunks - 1)
         for copy in to_z:
             copy.wait()
         total = bz_out[...]
@@ -337,12 +339,12 @@
     tok, hidden = grad_act.shape
     blocks = hidden // BLK
     steps = blocks // 2
-    chunks = 4
+    total_rows = weights.shape[1]
+    chunks = 8 if steps % 8 == 0 and total_rows % 128 == 0 else 4
     per = steps // chunks
-    total_rows = weights.shape[1]
     blk_rows = total_rows // blocks
     n = total_rows // chunks
-    strip = next(c for c in (160, 128, 96, 80, 64, 48, 32, 16) if n % c == 0)
+    strip = next(c for c in (240, 160, 128, 96, 80, 64, 48, 32, 16) if n % c == 0)
     rows = quads * 4
     whole = lambda a: pl.BlockSpec(a.shape, lambda i, p: (0, 0))
     wide = lambda m: pl.BlockSpec((m, 2 * BLK), lambda i, p: (0, pair_of(i, per, chunks)))

time: 231 us -> 204 us (0.88); the launches traced: 230 us -> 201 us
  Pallas kernels: 216 us -> 186 us
    pallas_call x1, Pallas kernels: 136 us -> 106 us  [fused(): pl.pallas_call(functools.partial(fused_kernel, quads, chunks, blk_rows, s...]
where the time goes in v3:
time: 204 us; the launch traced here: 201 us
  Pallas kernels  186 us (91%)
  local copies, waits for them, and re-layouts  14 us (7%)
    pallas_call x1, Pallas kernels, fused(): pl.pallas_call(functools.partial(fused_kernel, quads, chunks, blk_rows, s...  106 us
    pallas_call x1, Pallas kernels, gather(): pl.pallas_call(functools.partial(gather_kernel, quads), out_shape=(jax.Sh...  79.4 us
    unnamed x6, local copies, waits for them, and re-layouts  7.53 us

profile of v3, /device:TPU:9, one launch (start us, length us, event | category | flops | bytes accessed | tf_op | source)
XLA Modules:
  0.0 200.6 jit_solution(17686256916302844475)
XLA Ops:
  0.6 0.0 copy-start
  0.6 0.7 copy-done
  1.3 0.1 constant_dynamic-slice_fusion
  1.4 0.1 copy.8
  1.5 0.7 reshape.21.pat_ref
  2.2 1.3 reshape.23.bias_ref
  3.5 2.0 %reshape.22.w_ref = bf16[1920,128]{1,0:T(8,128)(2,1)} reshape(bf16[48,5120]{1,0:T(8,128)(2,1)} %param.6) | data formatting | bytes 983040 | tf_op jit(solution)/shard_map/reshape | solution.py:391
  5.5 79.4 %shard_map.76 = (bf16[16,1920,128]{2,1,0:T(8,128)(2,1)}, bf16[512,3072]{1,0:T(8,128)(2,1)}) custom-call(bf16[1920,128]{1,0:T(8,128)(2,1)} %reshape.22.w_ref, bf16[512,3072]{1,0:T(8,128)(2,1)} %own_ref.1), custom_call_target="tpu_custom_call" | custom-call | tf_op jit(solution)/shard_map/pallas_call | solution.py:145
  85.0 106.4 %shard_map.77 = (bf16[512,6144]{1,0:T(8,128)(2,1)}, f32[1920,128]{1,0:T(8,128)}, f32[48,128]{1,0:T(8,128)}) custom-call(s32[240]{0:T(256)} %reshape.21.pat_ref, bf16[512,3072]{1,0:T(8,128)(2,1)} %own_ref.1, bf16[512,3072]{1,0:T(8,128)(2,1)} %get-tuple-element.8.peer_ref, bf16[16,1920,128]{2,1,0:T(8,128)(2,1)} %get-tuple-element.9.w_ref, ...), custom_call_target="tpu_custom_call" | custom-call | tf_op jit(solution)/shard_map/pallas_call | solution.py:357
  191.4 2.3 %reshape.24 = f32[48,5120]{1,0:T(8,128)} reshape(f32[1920,128]{1,0:T(8,128)} %get-tuple-element.11) | data formatting | bytes 1966080 | tf_op jit(solution)/shard_map/reshape | solution.py:395
  193.7 0.0 copy-start.1
  193.7 6.2 %copy.11 = bf16[512,6144]{1,0:T(8,128)(2,1)} copy(bf16[512,6144]{1,0:T(8,128)(2,1)} %get-tuple-element.16) | data formatting | bytes 12582912
  200.0 0.0 copy-done.1
  200.0 0.6 copy.12
Async XLA Ops:
  0.6 0.7 copy-start
  193.7 6.2 %copy-start.1 = (f32[48,128]{1,0:T(8,128)S(1)}, f32[48,128]{1,0:T(8,128)}, u32[]{:S(2)}) copy-start(f32[48,128]{1,0:T(8,128)} %get-tuple-element.12) | copy-start | bytes 73732

commit v4 on v3

--- a/solution.py
+++ b/solution.py
@@ -103,25 +103,18 @@
     copies = []
     own = pltpu.make_async_copy(w_ref, all_ref.at[row], own_sem)
     own.start()
-    z_copies = []
-    for d in range(1, quads):
+    z_copies = {}
+
+    def send_quad(d):
         target = ((quad + d) % quads * 4 + bit_y * 2 + bit_x, col)
-        z_copies.append(send(w_ref, all_ref.at[row], z_s.at[d - 1], z_r.at[d - 1], target))
+        z_copies[d] = send(w_ref, all_ref.at[row], z_s.at[d - 1], z_r.at[d - 1], target)
+
+    order = sorted(range(quads), key=lambda d: min(d, quads - d))
+    send_quad(order[1])
     cut = [pl.ds(0, half), pl.ds(half, half)]
-    first_y, first_x = [], []
-    for d in range(quads):
-        src_row = (quad - d + quads) % quads * 4 + bit_y * 2 + bit_x
-        if d > 0:
-            z_copies[d - 1].wait_recv()
-        src = [w_ref.at[c] if d == 0 else all_ref.at[src_row, c] for c in cut]
-        dst = [all_ref.at[src_row, c] for c in cut]
-        first_y.append(send(src[0], dst[0], y_s.at[d], y_r.at[d], y_peer))
-        first_x.append(send(src[1], dst[1], x_s.at[d], x_r.at[d], x_peer))
-        copies.append(send(src[0], dst[0], x_s.at[quads + d], x_r.at[quads + d], x_peer))
-        copies.append(send(src[1], dst[1], y_s.at[quads + d], y_r.at[quads + d], y_peer))
-        if d == 0:
-            tok_copy = send(tok_ref, peer_ref, tok_s, tok_r, (row, 1 - col))
-    for d in range(quads):
+    first_y, first_x = {}, {}
+
+    def relay(d):
         from_quad = (quad - d + quads) % quads * 4
         y_row = from_quad + (1 - bit_y) * 2 + bit_x
         x_row = from_quad + bit_y * 2 + 1 - bit_x
@@ -131,9 +124,27 @@
         first_x[d].wait_recv()
         piece = all_ref.at[x_row, cut[1]]
         copies.append(send(piece, piece, y_s.at[2 * quads + d], y_r.at[2 * quads + d], y_peer))
+
+    for i, d in enumerate(order):
+        src_row = (quad - d + quads) % quads * 4 + bit_y * 2 + bit_x
+        if i > 0:
+            z_copies[d].wait_recv()
+            if i + 1 < quads:
+                send_quad(order[i + 1])
+        src = [w_ref.at[c] if d == 0 else all_ref.at[src_row, c] for c in cut]
+        dst = [all_ref.at[src_row, c] for c in cut]
+        first_y[d] = send(src[0], dst[0], y_s.at[d], y_r.at[d], y_peer)
+        first_x[d] = send(src[1], dst[1], x_s.at[d], x_r.at[d], x_peer)
+        copies.append(send(src[0], dst[0], x_s.at[quads + d], x_r.at[quads + d], x_peer))
+        copies.append(send(src[1], dst[1], y_s.at[quads + d], y_r.at[quads + d], y_peer))
+        if i == 0:
+            tok_copy = send(tok_ref, peer_ref, tok_s, tok_r, (row, 1 - col))
+        else:
+            relay(order[i - 1])
+    relay(order[-1])
     for copy in copies:
         copy.wait()
-    for copy in z_copies + first_y + first_x:
+    for copy in [*z_copies.values(), *first_y.values(), *first_x.values()]:
         copy.wait_send()
     tok_copy.wait()
     own.wait()

time: 204 us -> 188 us (0.922)
  Pallas kernels: 186 us -> 171 us
    pallas_call x1, Pallas kernels: 79.4 us -> 69.6 us  [gather(): pl.pallas_call(functools.partial(gather_kernel, quads), out_shape=(jax.Sh...]
    pallas_call x1, Pallas kernels: 106 us -> 102 us  [fused(): pl.pallas_call(functools.partial(fused_kernel, quads, chunks, blk_rows, s...]
where the time goes in v4:
time: 188 us; the launch traced here: 186 us
  Pallas kernels  171 us (91%)
  local copies, waits for them, and re-layouts  14 us (7%)
    pallas_call x1, Pallas kernels, fused(): pl.pallas_call(functools.partial(fused_kernel, quads, chunks, blk_rows, s...  102 us
    pallas_call x1, Pallas kernels, gather(): pl.pallas_call(functools.partial(gather_kernel, quads), out_shape=(jax.Sh...  69.6 us
    unnamed x6, local copies, waits for them, and re-layouts  7.53 us

profile of v4, /device:TPU:9, one launch (start us, length us, event | category | flops | bytes accessed | tf_op | source)
XLA Modules:
  0.0 185.8 jit_solution(6344416009363778227)
XLA Ops:
  0.6 0.0 copy-start
  0.6 0.7 copy-done
  1.3 0.1 constant_dynamic-slice_fusion
  1.4 0.1 copy.8
  1.5 0.7 reshape.21.pat_ref
  2.2 1.3 reshape.23.bias_ref
  3.5 2.0 %reshape.22.w_ref = bf16[1920,128]{1,0:T(8,128)(2,1)} reshape(bf16[48,5120]{1,0:T(8,128)(2,1)} %param.6) | data formatting | bytes 983040 | tf_op jit(solution)/shard_map/reshape | solution.py:402
  5.5 69.6 %shard_map.76 = (bf16[16,1920,128]{2,1,0:T(8,128)(2,1)}, bf16[512,3072]{1,0:T(8,128)(2,1)}) custom-call(bf16[1920,128]{1,0:T(8,128)(2,1)} %reshape.22.w_ref, bf16[512,3072]{1,0:T(8,128)(2,1)} %own_ref.1), custom_call_target="tpu_custom_call" | custom-call | tf_op jit(solution)/shard_map/pallas_call | solution.py:156
  75.1 101.5 %shard_map.77 = (bf16[512,6144]{1,0:T(8,128)(2,1)}, f32[1920,128]{1,0:T(8,128)}, f32[48,128]{1,0:T(8,128)}) custom-call(s32[240]{0:T(256)} %reshape.21.pat_ref, bf16[512,3072]{1,0:T(8,128)(2,1)} %own_ref.1, bf16[512,3072]{1,0:T(8,128)(2,1)} %get-tuple-element.8.peer_ref, bf16[16,1920,128]{2,1,0:T(8,128)(2,1)} %get-tuple-element.9.w_ref, ...), custom_call_target="tpu_custom_call" | custom-call | tf_op jit(solution)/shard_map/pallas_call | solution.py:368
  176.6 2.3 %reshape.24 = f32[48,5120]{1,0:T(8,128)} reshape(f32[1920,128]{1,0:T(8,128)} %get-tuple-element.11) | data formatting | bytes 1966080 | tf_op jit(solution)/shard_map/reshape | solution.py:406
  178.9 0.0 copy-start.1
  178.9 6.2 %copy.11 = bf16[512,6144]{1,0:T(8,128)(2,1)} copy(bf16[512,6144]{1,0:T(8,128)(2,1)} %get-tuple-element.16) | data formatting | bytes 12582912
  185.2 0.0 copy-done.1
  185.2 0.6 copy.12
Async XLA Ops:
  0.6 0.7 copy-start
  178.9 6.2 %copy-start.1 = (f32[48,128]{1,0:T(8,128)S(1)}, f32[48,128]{1,0:T(8,128)}, u32[]{:S(2)}) copy-start(f32[48,128]{1,0:T(8,128)} %get-tuple-element.12) | copy-start | bytes 73732
